TPU v7x, 512 devices: a whole 4x8x8 slice. The times are simulated.
512 devices in a mesh: vocab: 64 (over y, x, core), width: 8 (over z).
Axes of the slice: x: 4, y: 8, z: 8, core: 2. Of those that a mesh axis runs over, the one named last changes fastest.
Arguments:
- hidden: bfloat16 [8192, 2048], P('vocab', 'width'), may hold values from -400 to 400
- norm_gain: bfloat16 [2048], P('width'), may hold values from 0.5 to 1.5
- head_weight: bfloat16 [102400, 2048], P('vocab', 'width'), may hold values from -1 to 1
- targets: int32 [8192], P(('vocab', 'width')), may hold values from 0 to 102399
- pad_mask: int32 [8192], P(('vocab', 'width')), may hold values 0 or 1
- lengths: int32 [64], replicated, may hold values from 1 to 2048, 8192 in all
Outputs:
- entropy: float32 [8192], P(('vocab', 'width'))
- token_logprob: float32 [8192], P(('vocab', 'width'))
- seq_score: float32 [64], replicated
Inputs may be any that keep to these rules, and one draw needn't show every extreme that they name: The lengths sum to 8192.
All inputs are finite; a program needn't handle non-finite values. No bound on the sum of `pad_mask` on one device may be relied on, other than what follows from the above.
Results may differ from a plain program's by a relative error of at most 0.0031.
Values may be sent and summed in bfloat16 or wider, within the bound.
A program may use at most 64 MiB of HBM per device.

v0:
```python
import math
import jax
import jax.numpy as jnp
from jax import lax
from jax.sharding import PartitionSpec as P

epsilon = 1e-06


def merged_2(value, axis, join):
    pieces = jax.tree.map(lambda part: lax.all_gather(part, axis), value)
    head = jax.tree.map(lambda part: part[0], pieces)
    tail = jax.tree.map(lambda part: part[1:], pieces)
    total, _ = lax.scan(lambda total, piece: (join(total, piece), None), head, tail)
    return total


def summarize(logits, block_ids, first_col):
    peak = jnp.max(logits, axis=1)
    shifted = logits - peak[:, None]
    weights = jnp.exp(shifted)
    exp_total = jnp.sum(weights, axis=1)
    spread = jnp.sum(weights * shifted, axis=1)
    columns = first_col + lax.iota(jnp.int32, logits.shape[1])
    target_logit = jnp.sum(jnp.where(columns[None, :] == block_ids[:, None], logits, 0.0), axis=1)
    return (peak, exp_total, spread, target_logit)


def combine(earlier, later):
    peak = jnp.maximum(earlier[0], later[0])
    left_lift = jnp.exp(earlier[0] - peak)
    right_lift = jnp.exp(later[0] - peak)
    exp_total = earlier[1] * left_lift + later[1] * right_lift
    spread = left_lift * (earlier[2] + (earlier[0] - peak) * earlier[1]) + right_lift * (
        later[2] + (later[0] - peak) * later[1]
    )
    return (peak, exp_total, spread, earlier[3] + later[3])


def per_device(hidden, norm_gain, head_weight, targets, pad_mask, lengths):
    width_count = lax.axis_size("width")
    own_count = targets.shape[0]
    values = hidden.astype(jnp.float32)
    energy = lax.psum(jnp.sum(values * values, axis=1), "width")
    inv_rms = lax.rsqrt(energy / (hidden.shape[1] * width_count) + epsilon)
    normed = (values * inv_rms[:, None] * norm_gain.astype(jnp.float32)[None, :]).astype(
        jnp.bfloat16
    )
    full_rows = lax.all_to_all(normed, "width", split_axis=0, concat_axis=1, tiled=True)
    gathered, gathered_ids = (
        lax.all_gather(full_rows, "vocab", axis=0, tiled=True),
        lax.all_gather(targets, "vocab", axis=0, tiled=True),
    )
    col_count = head_weight.shape[0]
    first_col = lax.axis_index("vocab") * col_count
    total_rows = gathered.shape[0]
    block_rows = math.gcd(total_rows, 512)
    contract = (((1,), (1,)), ((), ()))
    head_full = lax.all_gather(head_weight, "width", axis=1, tiled=True)

    def per_block(inputs):
        logits = lax.dot_general(inputs[0], head_full, contract, preferred_element_type=jnp.float32)
        return summarize(logits, inputs[1], first_col)

    blocked = lax.map(
        per_block,
        (gathered.reshape(-1, block_rows, gathered.shape[1]), gathered_ids.reshape(-1, block_rows)),
    )
    statistics = (
        blocked[0].reshape(-1),
        blocked[1].reshape(-1),
        blocked[2].reshape(-1),
        blocked[3].reshape(-1),
    )
    merged = merged_2(statistics, "vocab", combine)
    own_start = lax.axis_index("vocab") * own_count
    peak = lax.dynamic_slice_in_dim(merged[0], own_start, own_count, 0)
    exp_total = lax.dynamic_slice_in_dim(merged[1], own_start, own_count, 0)
    spread = lax.dynamic_slice_in_dim(merged[2], own_start, own_count, 0)
    target_logit = lax.dynamic_slice_in_dim(merged[3], own_start, own_count, 0)
    kept_mask = pad_mask.astype(jnp.float32)
    log_total = jnp.log(exp_total)
    entropy = kept_mask * (log_total - spread / exp_total)
    token_logprob = kept_mask * (target_logit - peak - log_total)
    device_index = lax.axis_index("vocab") * width_count + lax.axis_index("width")
    token_index = device_index * own_count + lax.iota(jnp.int32, own_count)
    seq_ends = jnp.cumsum(lengths)
    seq_starts = seq_ends - lengths
    member = (
        (token_index[:, None] >= seq_starts[None, :]) & (token_index[:, None] < seq_ends[None, :])
    ).astype(jnp.float32)
    partial_value = jnp.sum(member * token_logprob[:, None], axis=0)
    seq_score = lax.psum(partial_value, ("vocab", "width")) / lengths.astype(jnp.float32)
    return (entropy, token_logprob, seq_score)


def solution(mesh):
    placed = (
        P("vocab", "width"),
        P("width"),
        P("vocab", "width"),
        P(("vocab", "width")),
        P(("vocab", "width")),
        P(),
    )
    return jax.shard_map(
        per_device,
        mesh=mesh,
        in_specs=placed,
        out_specs=(P(("vocab", "width")), P(("vocab", "width")), P()),
        check_vma=False,
    )
```

profile of v0, /device:TPU:1, one launch (start us, length us, event | category | flops | bytes accessed | tf_op | source)
XLA Modules:
  0.0 491.1 jit_solution(4575408305845917003)
XLA Ops:
  7.2 0.9 fusion.5
  8.2 20.3 %psum.14 = f32[128]{0:T(128)S(1)} all-reduce(f32[128]{0:T(128)S(1)} %fusion.5), channel_id=1, replica_groups=mesh['vocab'=64,'width'=8] {'width'}, use_global_device_ids=true, to_apply=%region_1.0 | all-reduce | flops 128 | bytes 1024 | tf_op jit(solution)/shard_map/psum | solution.py:44
  28.4 0.7 convert_element_type.18
  29.1 0.9 fusion.7
  30.0 9.6 %all_to_all.19 = bf16[8,16,256]{2,1,0:T(8,128)(2,1)S(1)} all-to-all(bf16[8,16,256]{2,1,0:T(8,128)(2,1)S(1)} %bitcast.73), channel_id=1, replica_groups=mesh['vocab'=64,'width'=8] {'width'}, dimensions={0} | all-to-all | bytes 131072 | tf_op jit(solution)/shard_map/all_to_all | solution.py:49
  40.3 0.7 all-gather.9.cloned.1.call-update
  41.1 1.3 dynamic-slice
  43.0 0.9 dynamic-update-slice
  43.9 22.5 %all-reduce = s32[1024]{0:T(1024)S(1)} all-reduce(s32[1024]{0:T(1024)S(1)} %dynamic-update-slice), channel_id=1, replica_groups=mesh['vocab'=64,'width'=8] {'vocab'}, use_global_device_ids=true, to_apply=%add | all-reduce | flops 1024 | bytes 8192
  66.4 0.7 copy.16
  67.4 0.7 sub.31
  68.0 58.4 %all-gather.7.cloned.1.call-done = bf16[1024,2048]{1,0:T(8,128)(2,1)} async-done(((bf16[16,2048]{1,0:T(8,128)(2,1)}), bf16[1024,2048]{1,0:T(8,128)(2,1)}) %all-gather.7.cloned.1.call-update) | async-done | bytes 4194320 | tf_op jit(solution)/shard_map/all_gather | solution.py:51
  126.4 83.2 %all-gather.9.cloned.1.call-done = bf16[1600,2048]{1,0:T(8,128)(2,1)} async-done(((bf16[1600,256]{1,0:T(8,128)(2,1)}), bf16[1600,2048]{1,0:T(8,128)(2,1)}) %all-gather.9.cloned.1.call-update) | async-done | bytes 6553616 | tf_op jit(solution)/shard_map/all_gather | solution.py:59
  209.6 16.2 %while.32 = (s32[]{:T(128)}, f32[2,512]{1,0:T(2,128)S(1)}, f32[2,512]{1,0:T(2,128)S(1)}, f32[2,512]{1,0:T(2,128)S(1)}, f32[2,512]{1,0:T(2,128)S(1)}, /*index=5*/...) while((s32[]{:T(128)}, f32[2,512]{1,0:T(2,128)S(1)}, ...), condition=%wide.region_7.8_spmd, body=%wide.region_2.7_spmd.sunk | while | flops 3361996288 | bytes 15250565 | solution.py:65
  209.6 6.4 %fusion.14 = (f32[512]{0:T(512)S(1)}, f32[512,1600]{0,1:T(8,128)S(1)}) fusion(bf16[1600,2048]{1,0:T(8,128)(2,1)} %get-tuple-element.320, bf16[2,512,2048]{2,1,0:T(8,128)(2,1)} %get-tuple-element.319, s32[]{:T(128)} %get-tuple-element.303), kind=kOutput, calls=%fused_computation.31.clone.1 | convolution fusion | flops 3356261888 | bytes 11930112 | tf_op jit(solution)/shard_map/while/body/eval_jaxpr/dot_general | solution.py:62
  216.1 1.4 fusion.15
  217.7 6.4 %fusion.14 = (f32[512]{0:T(512)S(1)}, f32[512,1600]{0,1:T(8,128)S(1)}) fusion(bf16[1600,2048]{1,0:T(8,128)(2,1)} %get-tuple-element.320, bf16[2,512,2048]{2,1,0:T(8,128)(2,1)} %get-tuple-element.319, s32[]{:T(128)} %get-tuple-element.303), kind=kOutput, calls=%fused_computation.31.clone.1 | convolution fusion | flops 3356261888 | bytes 11930112 | tf_op jit(solution)/shard_map/while/body/eval_jaxpr/dot_general | solution.py:62
  224.2 1.4 fusion.15
  225.8 42.7 %all-gather = f32[64,1,1024]{2,1,0:T(1,128)S(1)} all-gather(f32[1,1,1024]{2,1,0:T(1,128)S(1)} %reshape.60), channel_id=1, replica_groups=mesh['vocab'=64,'width'=8] {'vocab'}, dimensions={0}, use_global_device_ids=true | all-gather | bytes 266240 | tf_op jit(solution)/shard_map/all_gather | solution.py:11
  268.6 37.2 %all-gather.1 = f32[64,1,1024]{2,1,0:T(1,128)S(1)} all-gather(f32[1,1,1024]{2,1,0:T(1,128)S(1)} %reshape.62), channel_id=1, replica_groups=mesh['vocab'=64,'width'=8] {'vocab'}, dimensions={0}, use_global_device_ids=true | all-gather | bytes 266240 | tf_op jit(solution)/shard_map/all_gather | solution.py:11
  305.8 36.9 %all-gather.2 = f32[64,1,1024]{2,1,0:T(1,128)S(1)} all-gather(f32[1,1,1024]{2,1,0:T(1,128)S(1)} %reshape.64), channel_id=1, replica_groups=mesh['vocab'=64,'width'=8] {'vocab'}, dimensions={0}, use_global_device_ids=true | all-gather | bytes 266240 | tf_op jit(solution)/shard_map/all_gather | solution.py:11
  342.7 37.1 %all-gather.3 = f32[64,1,1024]{2,1,0:T(1,128)S(1)} all-gather(f32[1,1,1024]{2,1,0:T(1,128)S(1)} %reshape.66), channel_id=1, replica_groups=mesh['vocab'=64,'width'=8] {'vocab'}, dimensions={0}, use_global_device_ids=true | all-gather | bytes 266240 | tf_op jit(solution)/shard_map/all_gather | solution.py:11
  380.2 7.6 %while.33 = (s32[]{:T(128)}, f32[1024]{0:T(1024)S(1)}, f32[1024]{0:T(1024)S(1)}, f32[1024]{0:T(1024)S(1)}, f32[1024]{0:T(1024)S(1)}, /*index=5*/f32[63,1024]{1,0...) while((s32[]{:T(128)}, f32[1024]{0:T(1024)S(1)}, ...), condition=%wide.region_9.10_spmd, body=%wide.region_8.9_spmd.sunk | while | flops 16386 | bytes 110701 | solution.py:14
  388.4 95.3 %psum.15 = f32[64]{0:T(128)S(1)} all-reduce(f32[64]{0:T(128)S(1)} %select_reduce_fusion.1), channel_id=1, replica_groups=mesh['vocab'=64,'width'=8] {'vocab','width'}, use_global_device_ids=true, to_apply=%region_12.13 | all-reduce | flops 64 | bytes 512 | tf_op jit(solution)/shard_map/psum | solution.py:93
  (429 shorter events, 6.7 us)
Async XLA Ops:
  7.2 119.3 %all-gather.7.cloned.1.call-start = ((), (), s32[]{:S(2)}) async-start(), calls=%async_computation.1 | async-start | bytes 4259840 | tf_op jit(solution)/shard_map/all_gather | solution.py:51
  40.3 169.3 %all-gather.9.cloned.1.call-start = ((), (), s32[]{:S(2)}) async-start(), calls=%async_computation.2 | async-start | bytes 7372800 | tf_op jit(solution)/shard_map/all_gather | solution.py:59
  225.8 162.0 %copy-start.2 = (s32[16]{0:T(128)S(1)}, s32[16]{0:T(128)}, u32[]{:S(2)}) copy-start(s32[16]{0:T(128)} %param.14) | copy-start | bytes 196
  225.8 257.9 %copy-start.1 = (s32[64]{0:T(128)S(1)}, s32[64]{0:T(128)}, u32[]{:S(2)}) copy-start(s32[64]{0:T(128)} %param.15) | copy-start | bytes 772
  388.3 95.9 %copy-start = (f32[16]{0:T(128)}, f32[16]{0:T(128)S(1)}, u32[]{:S(2)}) copy-start(f32[16]{0:T(128)S(1)} %get-tuple-element.158) | copy-start | bytes 196
Sparse Core Ops, SparseCore 0:
  40.4 85.9 all-gather.6
  128.4 81.1 all-gather.8
where the time goes:
time: 491 us
  blocking collectives  302 us (62%)
  waiting for transfers between devices  142 us (29%)
  between operations  14.9 us (3%)
  matrix products  12.9 us (3%)
  other arithmetic  9.19 us (2%)
  local copies, waits for them, and re-layouts  6.36 us (1%)
    all_gather x4, blocking collectives, merged_2(): pieces = jax.tree.map(lambda part: lax.all_gather(part, axis), value)  154 us
    psum x1, blocking collectives, per_device(): lax.psum(partial_value, ('vocab', 'width')) / lengths.astype(jnp.float32)  95.3 us
    all_gather x1, waiting for transfers between devices, per_device(): head_full = lax.all_gather(head_weight, 'width', axis=1, tiled=True)  83.2 us
    all_gather x1, waiting for transfers between devices, per_device(): lax.all_gather(full_rows, 'vocab', axis=0, tiled=True)  58.4 us
    unnamed x1, blocking collectives  22.5 us
    psum x1, blocking collectives, per_device(): energy = lax.psum(jnp.sum(values * values, axis=1), 'width')  20.3 us
    dot_general x2, matrix products, per_block(): lax.dot_general(inputs[0], head_full, contract, preferred_element_type=jn...  12.9 us
  transfers between devices with their start and end apart: 2, of which 2 were waited for; matrix products, arithmetic and copies ran while one was open for 1% of the time, Pallas kernels for 0%

commit v1 on v0

--- a/solution.py
+++ b/solution.py
@@ -1,3 +1,4 @@
+import functools
 import math
 import jax
 import jax.numpy as jnp
@@ -5,6 +6,18 @@
 from jax.sharding import PartitionSpec as P
 
 epsilon = 1e-06
+
+
+def bring_side(vals, across):
+    return jnp.concatenate(
+        lax.all_to_all(
+            jnp.stack(lax.psum(1, across) * [vals], axis=0), across, split_axis=0, concat_axis=0
+        ),
+        axis=0,
+    )
+
+
+end_shifts_all_in = functools.partial(bring_side, across="vocab")
 
 
 def merged_2(value, axis, join):
@@ -48,7 +61,7 @@
     )
     full_rows = lax.all_to_all(normed, "width", split_axis=0, concat_axis=1, tiled=True)
     gathered, gathered_ids = (
-        lax.all_gather(full_rows, "vocab", axis=0, tiled=True),
+        end_shifts_all_in(full_rows),
         lax.all_gather(targets, "vocab", axis=0, tiled=True),
     )
     col_count = head_weight.shape[0]

time: 491 us -> 437 us (0.89)
  waiting for transfers between devices: 142 us -> 0.7 us
  blocking collectives: 302 us -> 373 us
  starting transfers between devices: 0.08 us -> 16 us
    all_gather x1, waiting for transfers between devices: 83.2 us -> 0.02 us  [per_device(): head_full = lax.all_gather(head_weight, 'width', axis=1, tiled=True)]
    unnamed x1, blocking collectives: 22.5 us -> 96.5 us
    all_gather x1 -> x0, waiting for transfers between devices: 58.4 us -> none  [per_device(): lax.all_gather(full_rows, 'vocab', axis=0, tiled=True)]
    all_to_all x0 -> x1, starting transfers between devices: none -> 16 us  [bring_side(): lax.all_to_all(jnp.stack(lax.psum(1, across) * [vals], axis=0), across, s...]
  transfers between devices with their start and end apart: 2 -> 2, of which waited for: 2 -> 0; matrix products, arithmetic and copies ran while one was open for 1% -> 2% of each run, Pallas kernels for 0% -> 0%
where the time goes in v1:
time: 437 us
  blocking collectives  373 us (85%)
  starting transfers between devices  16 us (4%)
  between operations  14.9 us (3%)
  matrix products  12.9 us (3%)
  other arithmetic  8.54 us (2%)
  local copies, waits for them, and re-layouts  7.05 us (2%)
    all_gather x4, blocking collectives, merged_2(): pieces = jax.tree.map(lambda part: lax.all_gather(part, axis), value)  151 us
    unnamed x1, blocking collectives  96.5 us
    psum x1, blocking collectives, per_device(): lax.psum(partial_value, ('vocab', 'width')) / lengths.astype(jnp.float32)  94.6 us
    psum x1, blocking collectives, per_device(): energy = lax.psum(jnp.sum(values * values, axis=1), 'width')  20.3 us
    all_to_all x1, starting transfers between devices, bring_side(): lax.all_to_all(jnp.stack(lax.psum(1, across) * [vals], axis=0), across, s...  16 us
    dot_general x2, matrix products, per_block(): lax.dot_general(inputs[0], head_full, contract, preferred_element_type=jn...  12.9 us
    all_to_all x1, blocking collectives, per_device(): lax.all_to_all(normed, 'width', split_axis=0, concat_axis=1, tiled=True)  10.3 us
  transfers between devices with their start and end apart: 2, of which 0 were waited for; matrix products, arithmetic and copies ran while one was open for 2% of the time, Pallas kernels for 0%

profile of v1, /device:TPU:1, one launch (start us, length us, event | category | flops | bytes accessed | tf_op | source)
XLA Modules:
  0.0 436.7 jit_solution(9345876188455136609)
XLA Ops:
  7.2 0.7 all-gather.6.cloned.1.call-update
  7.9 0.7 convert_element_type.18
  8.6 0.9 fusion.5
  9.5 20.3 %psum.14 = f32[128]{0:T(128)S(1)} all-reduce(f32[128]{0:T(128)S(1)} %fusion.5), channel_id=1, replica_groups=mesh['vocab'=64,'width'=8] {'width'}, use_global_device_ids=true, to_apply=%region_1.0 | all-reduce | flops 128 | bytes 1024 | tf_op jit(solution)/shard_map/psum | solution.py:57
  29.8 0.9 fusion.7
  30.7 10.3 %all_to_all.21 = bf16[8,16,256]{2,1,0:T(8,128)(2,1)S(1)} all-to-all(bf16[8,16,256]{2,1,0:T(8,128)(2,1)S(1)} %bitcast.73), channel_id=1, replica_groups=mesh['vocab'=64,'width'=8] {'width'}, dimensions={0} | all-to-all | bytes 131072 | tf_op jit(solution)/shard_map/all_to_all | solution.py:62
  41.0 2.6 stack.5
  43.6 16.0 %all-to-all-start.1 = ((bf16[64,16,2048]{2,1,0:T(8,128)(2,1)}), bf16[64,16,2048]{2,1,0:T(8,128)(2,1)}, u32[]{:S(2)}, u32[]{:S(2)}) async-start(bf16[64,16,2048]{2,1,0:T(8,128)(2,1)} %stack.5), calls=%async_computation.1 | async-start | bytes 8388608 | tf_op jit(solution)/shard_map/all_to_all | solution.py:13
  59.6 1.3 dynamic-slice
  61.5 0.2 dynamic-update-slice
  61.8 96.5 %all-reduce = s32[1024]{0:T(1024)S(1)} all-reduce(s32[1024]{0:T(1024)S(1)} %dynamic-update-slice), channel_id=1, replica_groups=mesh['vocab'=64,'width'=8] {'vocab'}, use_global_device_ids=true, to_apply=%add | all-reduce | flops 1024 | bytes 8192
  158.6 16.2 %while.32 = (s32[]{:T(128)}, f32[2,512]{1,0:T(2,128)S(1)}, f32[2,512]{1,0:T(2,128)S(1)}, f32[2,512]{1,0:T(2,128)S(1)}, f32[2,512]{1,0:T(2,128)S(1)}, /*index=5*/...) while((s32[]{:T(128)}, f32[2,512]{1,0:T(2,128)S(1)}, ...), condition=%wide.region_7.8_spmd, body=%wide.region_2.7_spmd.sunk | while | flops 3361996288 | bytes 15250565 | solution.py:78
  158.6 6.4 %fusion.14 = (f32[512]{0:T(512)S(1)}, f32[512,1600]{0,1:T(8,128)S(1)}) fusion(bf16[1600,2048]{1,0:T(8,128)(2,1)} %get-tuple-element.320, bf16[2,512,2048]{2,1,0:T(8,128)(2,1)} %get-tuple-element.319, s32[]{:T(128)} %get-tuple-element.303), kind=kOutput, calls=%fused_computation.31.clone.1 | convolution fusion | flops 3356261888 | bytes 11930112 | tf_op jit(solution)/shard_map/while/body/eval_jaxpr/dot_general | solution.py:75
  165.1 1.4 fusion.15
  166.7 6.4 %fusion.14 = (f32[512]{0:T(512)S(1)}, f32[512,1600]{0,1:T(8,128)S(1)}) fusion(bf16[1600,2048]{1,0:T(8,128)(2,1)} %get-tuple-element.320, bf16[2,512,2048]{2,1,0:T(8,128)(2,1)} %get-tuple-element.319, s32[]{:T(128)} %get-tuple-element.303), kind=kOutput, calls=%fused_computation.31.clone.1 | convolution fusion | flops 3356261888 | bytes 11930112 | tf_op jit(solution)/shard_map/while/body/eval_jaxpr/dot_general | solution.py:75
  173.2 1.4 fusion.15
  174.9 40.3 %all-gather = f32[64,1,1024]{2,1,0:T(1,128)S(1)} all-gather(f32[1,1,1024]{2,1,0:T(1,128)S(1)} %reshape.59), channel_id=1, replica_groups=mesh['vocab'=64,'width'=8] {'vocab'}, dimensions={0}, use_global_device_ids=true | all-gather | bytes 266240 | tf_op jit(solution)/shard_map/all_gather | solution.py:24
  215.2 36.9 %all-gather.1 = f32[64,1,1024]{2,1,0:T(1,128)S(1)} all-gather(f32[1,1,1024]{2,1,0:T(1,128)S(1)} %reshape.61), channel_id=1, replica_groups=mesh['vocab'=64,'width'=8] {'vocab'}, dimensions={0}, use_global_device_ids=true | all-gather | bytes 266240 | tf_op jit(solution)/shard_map/all_gather | solution.py:24
  252.1 37.2 %all-gather.2 = f32[64,1,1024]{2,1,0:T(1,128)S(1)} all-gather(f32[1,1,1024]{2,1,0:T(1,128)S(1)} %reshape.63), channel_id=1, replica_groups=mesh['vocab'=64,'width'=8] {'vocab'}, dimensions={0}, use_global_device_ids=true | all-gather | bytes 266240 | tf_op jit(solution)/shard_map/all_gather | solution.py:24
  289.3 36.9 %all-gather.3 = f32[64,1,1024]{2,1,0:T(1,128)S(1)} all-gather(f32[1,1,1024]{2,1,0:T(1,128)S(1)} %reshape.65), channel_id=1, replica_groups=mesh['vocab'=64,'width'=8] {'vocab'}, dimensions={0}, use_global_device_ids=true | all-gather | bytes 266240 | tf_op jit(solution)/shard_map/all_gather | solution.py:24
  326.5 7.6 %while.33 = (s32[]{:T(128)}, f32[1024]{0:T(1024)S(1)}, f32[1024]{0:T(1024)S(1)}, f32[1024]{0:T(1024)S(1)}, f32[1024]{0:T(1024)S(1)}, /*index=5*/f32[63,1024]{1,0...) while((s32[]{:T(128)}, f32[1024]{0:T(1024)S(1)}, ...), condition=%wide.region_9.10_spmd, body=%wide.region_8.9_spmd.sunk | while | flops 16386 | bytes 110701 | solution.py:27
  334.1 0.6 subtract_multiply_fusion
  334.8 94.6 %psum.15 = f32[64]{0:T(128)S(1)} all-reduce(f32[64]{0:T(128)S(1)} %select_reduce_fusion.1), channel_id=1, replica_groups=mesh['vocab'=64,'width'=8] {'vocab','width'}, use_global_device_ids=true, to_apply=%region_12.13 | all-reduce | flops 64 | bytes 512 | tf_op jit(solution)/shard_map/psum | solution.py:106
  429.4 0.5 convert_divide_fusion
  (431 shorter events, 5.1 us)
Async XLA Ops:
  7.2 151.5 %all-gather.6.cloned.1.call-start = ((), (), s32[]{:S(2)}) async-start(), calls=%async_computation.2 | async-start | bytes 7372800 | tf_op jit(solution)/shard_map/all_gather | solution.py:72
  43.6 18.0 %copy-start.3 = (s32[16]{0:T(128)S(1)}, s32[16]{0:T(128)}, u32[]{:S(2)}) copy-start(s32[16]{0:T(128)} %param.13) | copy-start | bytes 196
  43.6 114.7 %copy-start.1 = (s32[64]{0:T(128)S(1)}, s32[64]{0:T(128)}, u32[]{:S(2)}) copy-start(s32[64]{0:T(128)} %param.15) | copy-start | bytes 772
  43.6 115.0 %all-to-all-start.1 = ((bf16[64,16,2048]{2,1,0:T(8,128)(2,1)}), bf16[64,16,2048]{2,1,0:T(8,128)(2,1)}, u32[]{:S(2)}, u32[]{:S(2)}) async-start(bf16[64,16,2048]{2,1,0:T(8,128)(2,1)} %stack.5), calls=%async_computation.1 | async-start | bytes 8388608 | tf_op jit(solution)/shard_map/all_to_all | solution.py:13
  174.8 159.3 %copy-start.2 = (s32[16]{0:T(128)S(1)}, s32[16]{0:T(128)}, u32[]{:S(2)}) copy-start(s32[16]{0:T(128)} %param.14) | copy-start | bytes 196
  334.7 95.2 %copy-start = (f32[16]{0:T(128)}, f32[16]{0:T(128)S(1)}, u32[]{:S(2)}) copy-start(f32[16]{0:T(128)S(1)} %get-tuple-element.158) | copy-start | bytes 196
Sparse Core Ops, SparseCore 0:
  10.0 90.4 all-gather.5
